TPU v7x, 256 devices: a whole 4x4x8 slice. The times are simulated.
256 devices in a mesh: tm: 8 (over y, core), vert: 32 (over z, x).
Axes of the slice: x: 4, y: 4, z: 8, core: 2. Of those that a mesh axis runs over, the one named last changes fastest.
Arguments:
- features: bfloat16 [32, 16384, 128], P('tm', 'vert'), may hold values from -6 to 6
- tile_cols: int32 [32, 128, 8], P('tm', 'vert'), may hold values from 0 to 127, as said below
- tile_vals: bfloat16 [32, 128, 8, 128, 128], P('tm', 'vert'), may hold values from -0.1875 to 0.1875
- space_weight: bfloat16 [128, 128], replicated, may hold values from -0.5 to 0.5
- positions: bfloat16 [32, 128], replicated, may hold values from -6 to 6
- attn_proj: bfloat16 [128, 384], replicated, may hold values from -0.5 to 0.5
- attn_out: bfloat16 [128, 128], replicated, may hold values from -0.5 to 0.5
- norm_gain: float32 [128], replicated, may hold values from 0.1 to 1.9
- mlp_up: bfloat16 [128, 512], replicated, may hold values from -0.5 to 0.5
- mlp_down: bfloat16 [512, 128], replicated, may hold values from -0.25 to 0.25
Outputs:
- embedded: bfloat16 [32, 16384, 128], P('tm', 'vert')
Inputs may be any that keep to these rules, and one draw needn't show every extreme that they name: `tile_cols`: for each snapshot and each group of 4 consecutive row blocks, the listed column blocks name at most two distinct blocks among those of any one group (blocks c with the same c // 4), and exactly two for some group.
All inputs are finite; a program needn't handle non-finite values.
Results may differ from a plain program's by a relative error of at most 0.0064.
Values may be sent and summed in bfloat16 or wider, within the bound.
A program may use at most 128 MiB of HBM per device.

v0:
```python
import math
import jax
import jax.numpy as jnp
from jax import lax
from jax.sharding import PartitionSpec as P

HEADS = 16
cap_value = 4.0
norm_eps = 1e-05


def temporal(hidden, positions, attn_proj, attn_out, norm_gain, mlp_up, mlp_down):
    snap_total = hidden.shape[0]
    feature_dim = hidden.shape[2]
    head_count = HEADS
    head_dim = feature_dim // head_count
    mixed_in = (hidden.astype(jnp.float32) + positions.astype(jnp.float32)[:, None, :]).astype(
        jnp.bfloat16
    )
    flat_in = mixed_in.reshape(-1, feature_dim)
    projected = jnp.dot(flat_in, attn_proj, preferred_element_type=jnp.float32).astype(jnp.bfloat16)
    projected = projected.reshape(snap_total, -1, 3, head_count, head_dim)
    query_part = projected[:, :, 0]
    key_part = projected[:, :, 1]
    value_part = projected[:, :, 2]
    scores = jnp.einsum(
        "tvhd,uvhd->vhtu", query_part, key_part, preferred_element_type=jnp.float32
    ) / math.sqrt(head_dim)
    capped = cap_value * jnp.tanh(scores / cap_value)
    causal = jnp.arange(snap_total)[:, None] >= jnp.arange(snap_total)[None, :]
    raised = jnp.where(causal, jnp.exp(capped), 0.0)
    weights = (raised / jnp.sum(raised, axis=-1, keepdims=True)).astype(jnp.bfloat16)
    attended = jnp.einsum(
        "vhtu,uvhd->tvhd", weights, value_part, preferred_element_type=jnp.float32
    ).astype(jnp.bfloat16)
    stream = flat_in.astype(jnp.float32) + jnp.dot(
        attended.reshape(-1, feature_dim), attn_out, preferred_element_type=jnp.float32
    )
    centre = jnp.mean(stream, axis=-1, keepdims=True)
    spread = jnp.mean((stream - centre) ** 2, axis=-1, keepdims=True)
    normed = ((stream - centre) * lax.rsqrt(spread + norm_eps) * norm_gain).astype(jnp.bfloat16)
    expanded = jax.nn.relu(jnp.dot(normed, mlp_up, preferred_element_type=jnp.float32)).astype(
        jnp.bfloat16
    )
    output = stream + jnp.dot(expanded, mlp_down, preferred_element_type=jnp.float32)
    return output.astype(jnp.bfloat16).reshape(snap_total, -1, feature_dim)


def spatial(features, tile_cols, tile_vals, space_weight):
    snap_count, row_count, feature_dim = features.shape
    tile_size = tile_vals.shape[-1]
    block_count = row_count // tile_size
    tile_count = tile_cols.shape[2]
    flat_cols = tile_cols.reshape(snap_count, block_count * tile_count)
    everything = lax.all_gather(features, "vert", axis=1, tiled=True)
    everything = everything.reshape(snap_count, -1, tile_size, feature_dim)
    blocks = jnp.take_along_axis(everything, flat_cols[:, :, None, None], axis=1)
    blocks = blocks.reshape(snap_count, block_count, tile_count, tile_size, feature_dim)
    summed = jnp.einsum(
        "srkij,srkjd->srid", tile_vals, blocks, preferred_element_type=jnp.float32
    ).astype(jnp.bfloat16)
    hidden = jax.nn.relu(
        jnp.dot(summed.reshape(-1, feature_dim), space_weight, preferred_element_type=jnp.float32)
    )
    return hidden.astype(jnp.bfloat16).reshape(snap_count, row_count, feature_dim)


def local(
    features,
    tile_cols,
    tile_vals,
    space_weight,
    positions,
    attn_proj,
    attn_out,
    norm_gain,
    mlp_up,
    mlp_down,
):
    snap_count, row_count, feature_dim = features.shape
    time_count = lax.axis_size("tm")
    hidden = spatial(features, tile_cols, tile_vals, space_weight)
    grouped = hidden.reshape(snap_count, time_count, row_count // time_count, feature_dim)
    arrived = lax.all_to_all(grouped, "tm", split_axis=1, concat_axis=0, tiled=True)
    snap_total = arrived.shape[0]
    timeline = arrived.reshape(snap_total, -1, feature_dim)
    result = temporal(timeline, positions, attn_proj, attn_out, norm_gain, mlp_up, mlp_down)
    result = result.reshape(snap_total, 1, -1, feature_dim)
    embedded = lax.all_to_all(result, "tm", split_axis=0, concat_axis=1, tiled=True)
    return embedded.reshape(snap_count, row_count, feature_dim)


def solution(mesh):
    placed = (
        P("tm", "vert", None),
        P("tm", "vert", None),
        P("tm", "vert", None, None, None),
        P(),
        P(),
        P(),
        P(),
        P(),
        P(),
        P(),
    )
    return jax.shard_map(
        local, mesh=mesh, in_specs=placed, out_specs=P("tm", "vert", None), check_vma=False
    )
```

profile of v0, /device:TPU:1, one launch (start us, length us, event | category | flops | bytes accessed | tf_op | source)
XLA Modules:
  0.0 253.4 jit_solution(15430646949209116984)
XLA Ops:
  6.5 0.7 all-gather.2.cloned.1.call-update
  7.3 0.8 broadcast_in_dim_reshape.3
  8.1 0.1 reshape.115
  8.1 0.7 compare_and_fusion
  8.8 143.9 %all-gather.2.cloned.1.call-done = bf16[4,16384,128]{2,1,0:T(8,128)(2,1)} async-done(((bf16[4,512,128]{2,1,0:T(8,128)(2,1)}), bf16[4,16384,128]{2,1,0:T(8,128)(2,1)}) %all-gather.2.cloned.1.call-update) | async-done | bytes 16777232 | tf_op jit(solution)/shard_map/all_gather | solution.py:55
  152.7 8.8 %gather_fusion = bf16[128,128,128]{2,1,0:T(8,128)(2,1)} fusion(bf16[4,128,128,128]{3,2,1,0:T(8,128)(2,1)} %bitcast.66, s32[128]{0:T(128)S(1)} %reshape.115), kind=kCustom, calls=%fused_computation | custom fusion | bytes 8389632 | tf_op jit(solution)/shard_map/jit(take_along_axis)/gather | solution.py:57
  161.6 4.8 %fusion.17 = bf16[4,4,128,128]{2,3,1,0:T(8,128)(2,1)S(1)} fusion(bf16[4,4,8,128,128]{4,3,2,1,0:T(8,128)(2,1)} %param.12, bf16[4,4,8,128,128]{4,3,2,1,0:T(8,128)(2,1)} %bitcast.63, pred[4,4,8]{2,1,0:T(4,128)(4,1)S(1)} %compare_and_fusion), kind=kOutput, calls=%fused_computation.22 | convolution fusion | flops 539230208 | bytes 8913024 | tf_op jit(solution)/shard_map/srkij,srkjd->srid/dot_general | solution.py:59
  166.4 0.0 copy-start.5
  166.4 0.3 fusion.5
  166.7 0.8 copy.25
  167.5 5.7 %all-to-all-start = ((bf16[4,8,64,128]{3,2,0,1:T(8,128)(2,1)}), bf16[4,8,64,128]{3,2,0,1:T(8,128)(2,1)S(1)}, u32[]{:S(2)}, u32[]{:S(2)}) async-start(bf16[4,8,64,128]{3,2,0,1:T(8,128)(2,1)} %copy.25), calls=%async_computation | async-start | bytes 1048576 | tf_op jit(solution)/shard_map/all_to_all | solution.py:84
  173.2 9.3 %all-to-all-done = bf16[4,8,64,128]{3,2,0,1:T(8,128)(2,1)S(1)} async-done(((bf16[4,8,64,128]{3,2,0,1:T(8,128)(2,1)}), bf16[4,8,64,128]{3,2,0,1:T(8,128)(2,1)S(1)}, u32[]{:S(2)}, u32[]{:S(2)}) %all-to-all-start) | async-done | bytes 524320 | tf_op jit(solution)/shard_map/all_to_all | solution.py:84
  182.6 0.1 bitcast_convert_fusion
  182.7 0.1 fusion.20
  182.8 0.0 copy-start.1
  182.8 0.8 copy-done.1
  183.6 0.5 convolution_convert_fusion
  184.1 1.7 copy.26
  185.8 4.6 %reshape.110 = bf16[32,64,3,16,8]{1,0,4,3,2:T(8,128)(2,1)S(1)} reshape(bf16[2048,384]{0,1:T(8,128)(2,1)} %copy.26) | data formatting | bytes 3145728 | tf_op jit(solution)/shard_map/reshape | solution.py:22
  190.4 1.8 fusion.35
  192.2 4.3 %copy.37 = bf16[32,64,1,16,8]{0,4,3,1,2:T(8,128)(2,1)S(1)} copy(bf16[32,64,1,16,8]{1,0,4,3,2:T(8,128)(2,1)} %get-tuple-element.6) | data formatting | bytes 1048576
  196.5 4.9 %copy.38 = bf16[32,64,1,16,8]{0,4,3,1,2:T(8,128)(2,1)} copy(bf16[32,64,1,16,8]{1,0,4,3,2:T(8,128)(2,1)} %get-tuple-element.7) | data formatting | bytes 1048576
  201.3 3.9 %copy.36 = bf16[32,64,1,16,8]{0,4,3,1,2:T(8,128)(2,1)} copy(bf16[32,64,1,16,8]{1,0,4,3,2:T(8,128)(2,1)S(1)} %copy-done.3) | data formatting | bytes 1048576
  205.2 11.1 %fusion = (f32[64,16,32]{2,1,0:T(8,128)S(1)}, f32[64,16,32,32]{2,3,1,0:T(8,128)}) fusion(pred[32,32]{0,1:T(8,128)(4,1)S(1)} %iota_compare_fusion, bf16[32,64,1,16,8]{0,4,3,1,2:T(8,128)(2,1)} %copy.38, bf16[32,64,1,16,8]{0,4,3,1,2:T(8,128)(2,1)S(1)} %copy.37), kind=kOutput, calls=%fused_computation.3 | convolution fusion | flops 20938752 | bytes 5374976 | tf_op jit(solution)/shard_map/tvhd,uvhd->vhtu/dot_general | solution.py:26
  216.4 9.8 %convert_bitcast_fusion = bf16[32,64,16,8]{0,3,2,1:T(8,128)(2,1)} fusion(f32[64,16,32,32]{2,3,1,0:T(8,128)} %get-tuple-element.9, f32[64,16,32]{2,1,0:T(8,128)S(1)} %get-tuple-element.8, pred[32,32]{0,1:T(8,128)(4,1)S(1)} %iota_compare_fusion, bf16[32,64,1,16,8]{0,4,3,1,2:T(8,128)(2,1)S(1)} %copy-done.4), kind=kOutput, calls=%fused_computation.19 | convolution fusion | flops 22282240 | bytes 5374976 | tf_op jit(solution)/shard_map/vhtu,uvhd->tvhd/dot_general | solution.py:33
  226.2 3.4 %copy.31 = bf16[32,64,16,8]{1,0,3,2:T(8,128)(2,1)S(1)} copy(bf16[32,64,16,8]{0,3,2,1:T(8,128)(2,1)} %convert_bitcast_fusion) | data formatting | bytes 1048576 | tf_op jit(solution)/shard_map/convert_element_type | solution.py:35
  229.6 0.8 reshape.111
  230.4 0.6 fusion.36
  231.0 0.6 multiply_reduce_fusion
  231.7 1.3 fusion.6
  233.0 12.7 %all_to_all.24 = bf16[32,1,64,128]{3,2,1,0:T(8,128)(2,1)S(1)} all-to-all(bf16[32,1,64,128]{3,2,1,0:T(8,128)(2,1)S(1)} %bitcast.67), channel_id=1, replica_groups=mesh['tm'=8,'vert'=32] {'tm'}, dimensions={0} | all-to-all | bytes 1048576 | tf_op jit(solution)/shard_map/all_to_all | solution.py:89
  245.7 0.8 copy.33
  (25 shorter events, 0.1 us)
Async XLA Ops:
  6.5 225.1 %copy-start = (bf16[512,128]{1,0:T(8,128)(2,1)S(1)}, bf16[512,128]{1,0:T(8,128)(2,1)}, u32[]{:S(2)}) copy-start(bf16[512,128]{1,0:T(8,128)(2,1)} %param.19) | copy-start | bytes 393220
  6.5 146.2 %all-gather.2.cloned.1.call-start = ((), (), s32[]{:S(2)}) async-start(), calls=%async_computation.2 | async-start | bytes 17301504 | tf_op jit(solution)/shard_map/all_gather | solution.py:55
  161.6 4.8 %copy-start.7 = (bf16[128,128]{1,0:T(8,128)(2,1)S(1)}, bf16[128,128]{1,0:T(8,128)(2,1)}, u32[]{:S(2)}) copy-start(bf16[128,128]{1,0:T(8,128)(2,1)} %param.13) | copy-start | bytes 98308
  161.6 11.7 %copy-start.8 = (bf16[32,128]{1,0:T(8,128)(2,1)S(1)}, bf16[32,128]{1,0:T(8,128)(2,1)}, u32[]{:S(2)}) copy-start(bf16[32,128]{1,0:T(8,128)(2,1)} %param.14) | copy-start | bytes 24580
  166.4 17.2 %copy-start.5 = (bf16[128,384]{1,0:T(8,128)(2,1)S(1)}, bf16[128,384]{1,0:T(8,128)(2,1)}, u32[]{:S(2)}) copy-start(bf16[128,384]{1,0:T(8,128)(2,1)} %param.15) | copy-start | bytes 294916
  167.5 15.0 %all-to-all-start = ((bf16[4,8,64,128]{3,2,0,1:T(8,128)(2,1)}), bf16[4,8,64,128]{3,2,0,1:T(8,128)(2,1)S(1)}, u32[]{:S(2)}, u32[]{:S(2)}) async-start(bf16[4,8,64,128]{3,2,0,1:T(8,128)(2,1)} %copy.25), calls=%async_computation | async-start | bytes 1048576 | tf_op jit(solution)/shard_map/all_to_all | solution.py:84
  182.8 0.8 copy-start.1
  192.2 9.1 %copy-start.3 = (bf16[32,64,1,16,8]{1,0,4,3,2:T(8,128)(2,1)S(1)}, bf16[32,64,1,16,8]{1,0,4,3,2:T(8,128)(2,1)}, u32[]{:S(2)}) copy-start(bf16[32,64,1,16,8]{1,0,4,3,2:T(8,128)(2,1)} %get-tuple-element.5) | copy-start | bytes 1572868
  205.2 11.1 %copy-start.4 = (bf16[32,64,1,16,8]{0,4,3,1,2:T(8,128)(2,1)S(1)}, bf16[32,64,1,16,8]{0,4,3,1,2:T(8,128)(2,1)}, u32[]{:S(2)}) copy-start(bf16[32,64,1,16,8]{0,4,3,1,2:T(8,128)(2,1)} %copy.36) | copy-start | bytes 1572868
  226.1 4.2 %copy-start.2 = (bf16[2048,128]{1,0:T(8,128)(2,1)S(1)}, bf16[2048,128]{1,0:T(8,128)(2,1)}, u32[]{:S(2)}) copy-start(bf16[2048,128]{1,0:T(8,128)(2,1)} %copy-done.1) | copy-start | bytes 1572868
  226.1 4.2 %copy-start.6 = (bf16[128,128]{1,0:T(8,128)(2,1)S(1)}, bf16[128,128]{1,0:T(8,128)(2,1)}, u32[]{:S(2)}) copy-start(bf16[128,128]{1,0:T(8,128)(2,1)} %param.16) | copy-start | bytes 98308
  226.2 5.5 %copy-start.9 = (bf16[128,512]{1,0:T(8,128)(2,1)S(1)}, bf16[128,512]{1,0:T(8,128)(2,1)}, u32[]{:S(2)}) copy-start(bf16[128,512]{1,0:T(8,128)(2,1)} %param.18) | copy-start | bytes 393220
  226.2 5.5 %copy-start.10 = (f32[128]{0:T(128)S(1)}, f32[128]{0:T(128)}, u32[]{:S(2)}) copy-start(f32[128]{0:T(128)} %param.17) | copy-start | bytes 1540
Sparse Core Ops, SparseCore 0:
  9.9 142.7 all-gather.1
where the time goes:
time: 254 us; the launch traced here: 253 us
  waiting for transfers between devices  154 us (61%)
  local copies, waits for them, and re-layouts  37.5 us (15%)
  matrix products  28.4 us (11%)
  between operations  13.6 us (5%)
  blocking collectives  12.7 us (5%)
  starting transfers between devices  5.69 us (2%)
    all_gather x1, waiting for transfers between devices, spatial(): everything = lax.all_gather(features, 'vert', axis=1, tiled=True)  144 us
    unnamed x25, local copies, waits for them, and re-layouts  13.9 us
    all_to_all x1, blocking collectives, local(): lax.all_to_all(result, 'tm', split_axis=0, concat_axis=1, tiled=True)  12.7 us
    dot_general x1, matrix products, temporal(): jnp.einsum('tvhd,uvhd->vhtu', query_part, key_part, preferred_element_typ...  11.1 us
    dot_general x1, matrix products, temporal(): jnp.einsum('vhtu,uvhd->tvhd', weights, value_part, preferred_element_type...  9.77 us
    all_to_all x1, waiting for transfers between devices, local(): lax.all_to_all(grouped, 'tm', split_axis=1, concat_axis=0, tiled=True)  9.33 us
    gather x2, local copies, waits for them, and re-layouts, spatial(): jnp.take_along_axis(everything, flat_cols[:, :, None, None], axis=1)  8.93 us
    all_to_all x1, starting transfers between devices, local(): lax.all_to_all(grouped, 'tm', split_axis=1, concat_axis=0, tiled=True)  5.69 us
  transfers between devices with their start and end apart: 2, of which 2 were waited for; matrix products, arithmetic and copies ran while one was open for 1% of the time, Pallas kernels for 0%

commit v1 on v0

--- a/solution.py
+++ b/solution.py
@@ -52,7 +52,10 @@
     block_count = row_count // tile_size
     tile_count = tile_cols.shape[2]
     flat_cols = tile_cols.reshape(snap_count, block_count * tile_count)
-    everything = lax.all_gather(features, "vert", axis=1, tiled=True)
+    devices = lax.axis_size("vert")
+    pieces = jnp.stack([features for _ in range(devices)])
+    pieces = lax.all_to_all(pieces, "vert", split_axis=0, concat_axis=0)
+    everything = jnp.concatenate(pieces, axis=1)
     everything = everything.reshape(snap_count, -1, tile_size, feature_dim)
     blocks = jnp.take_along_axis(everything, flat_cols[:, :, None, None], axis=1)
     blocks = blocks.reshape(snap_count, block_count, tile_count, tile_size, feature_dim)

time: 254 us -> 534 us (2.10)
  the two profiles are of different devices: /device:TPU:1 before, /device:TPU:4 now
where the time goes in v1:
time: 534 us; the launch traced here: 533 us
  waiting for transfers between devices  417 us (78%)
  local copies, waits for them, and re-layouts  57.8 us (11%)
  matrix products  28.4 us (5%)
  starting transfers between devices  16.3 us (3%)
  blocking collectives  12.8 us (2%)
    all_to_all x1, waiting for transfers between devices, spatial(): pieces = lax.all_to_all(pieces, 'vert', split_axis=0, concat_axis=0)  407 us
    all_to_all x1, local copies, waits for them, and re-layouts, spatial(): pieces = lax.all_to_all(pieces, 'vert', split_axis=0, concat_axis=0)  13.9 us
    unnamed x27, local copies, waits for them, and re-layouts  13.9 us
    all_to_all x1, blocking collectives, local(): lax.all_to_all(result, 'tm', split_axis=0, concat_axis=1, tiled=True)  12.8 us
    all_to_all x1, starting transfers between devices, spatial(): pieces = lax.all_to_all(pieces, 'vert', split_axis=0, concat_axis=0)  11.8 us
    dot_general x1, matrix products, temporal(): jnp.einsum('tvhd,uvhd->vhtu', query_part, key_part, preferred_element_typ...  11.1 us
  transfers between devices with their start and end apart: 2, of which 2 were waited for; matrix products, arithmetic and copies ran while one was open for 0% of the time, Pallas kernels for 0%

profile of v1, /device:TPU:4, one launch (start us, length us, event | category | flops | bytes accessed | tf_op | source)
XLA Modules:
  0.0 533.1 jit_solution(11694064284142756954)
XLA Ops:
  0.0 7.1 %stack.2 = bf16[32,4,512,128]{3,2,1,0:T(8,128)(2,1)} broadcast(bf16[4,512,128]{2,1,0:T(8,128)(2,1)} %param.10), dimensions={1,2,3} | broadcast | bytes 17301504 | tf_op jit(solution)/shard_map/stack | solution.py:56
  7.1 11.8 %all-to-all-start = ((bf16[32,4,512,128]{3,2,1,0:T(8,128)(2,1)}), bf16[32,4,512,128]{3,2,1,0:T(8,128)(2,1)}, u32[]{:S(2)}, u32[]{:S(2)}) async-start(bf16[32,4,512,128]{3,2,1,0:T(8,128)(2,1)} %stack.2), calls=%async_computation | async-start | bytes 33554432 | tf_op jit(solution)/shard_map/all_to_all | solution.py:57
  18.9 0.1 broadcast_in_dim_reshape.3
  18.9 0.1 reshape.117
  19.1 406.5 %all-to-all-done = bf16[32,4,512,128]{3,2,1,0:T(8,128)(2,1)} async-done(((bf16[32,4,512,128]{3,2,1,0:T(8,128)(2,1)}), bf16[32,4,512,128]{3,2,1,0:T(8,128)(2,1)}, u32[]{:S(2)}, u32[]{:S(2)}) %all-to-all-start) | async-done | bytes 16777248 | tf_op jit(solution)/shard_map/all_to_all | solution.py:57
  425.6 13.9 %copy.25 = bf16[32,4,512,128]{3,2,0,1:T(8,128)(2,1)} copy(bf16[32,4,512,128]{3,2,1,0:T(8,128)(2,1)} %all-to-all-done) | data formatting | bytes 33554432 | tf_op jit(solution)/shard_map/all_to_all | solution.py:57
  439.5 8.8 %gather_fusion = bf16[128,128,128]{2,1,0:T(8,128)(2,1)} fusion(bf16[4,128,128,128]{3,2,1,0:T(8,128)(2,1)} %bitcast.65, s32[128]{0:T(128)S(1)} %reshape.117), kind=kCustom, calls=%fused_computation | custom fusion | bytes 8389632 | tf_op jit(solution)/shard_map/jit(take_along_axis)/gather | solution.py:60
  448.4 4.8 fusion.17
  453.2 0.0 copy-start.5
  453.2 0.3 fusion.5
  453.5 0.8 copy.26
  454.3 4.5 all-to-all-start.1
  458.8 10.3 %all-to-all-done.1 = bf16[4,8,64,128]{3,2,0,1:T(8,128)(2,1)S(1)} async-done(((bf16[4,8,64,128]{3,2,0,1:T(8,128)(2,1)}), bf16[4,8,64,128]{3,2,0,1:T(8,128)(2,1)S(1)}, u32[]{:S(2)}, u32[]{:S(2)}) %all-to-all-start.1) | async-done | bytes 524320 | tf_op jit(solution)/shard_map/all_to_all | solution.py:87
  469.1 0.1 bitcast_convert_fusion
  469.2 0.1 fusion.20
  469.3 0.8 copy-done.1
  470.1 0.6 convolution_convert_fusion
  470.7 1.7 copy.27
  472.4 4.6 reshape.112
  476.9 1.8 fusion.35
  478.7 4.3 copy.38
  483.0 4.9 copy.39
  487.9 3.9 copy.37
  491.8 11.1 %fusion = (f32[64,16,32]{2,1,0:T(8,128)S(1)}, f32[64,16,32,32]{2,3,1,0:T(8,128)}) fusion(pred[32,32]{0,1:T(8,128)(4,1)S(1)} %iota_compare_fusion, bf16[32,64,1,16,8]{0,4,3,1,2:T(8,128)(2,1)} %copy.39, bf16[32,64,1,16,8]{0,4,3,1,2:T(8,128)(2,1)S(1)} %copy.38), kind=kOutput, calls=%fused_computation.3 | convolution fusion | flops 20938752 | bytes 5374976 | tf_op jit(solution)/shard_map/tvhd,uvhd->vhtu/dot_general | solution.py:26
  502.9 9.8 %convert_bitcast_fusion = bf16[32,64,16,8]{0,3,2,1:T(8,128)(2,1)} fusion(f32[64,16,32,32]{2,3,1,0:T(8,128)} %get-tuple-element.9, f32[64,16,32]{2,1,0:T(8,128)S(1)} %get-tuple-element.8, pred[32,32]{0,1:T(8,128)(4,1)S(1)} %iota_compare_fusion, bf16[32,64,1,16,8]{0,4,3,1,2:T(8,128)(2,1)S(1)} %copy-done.4), kind=kOutput, calls=%fused_computation.19 | convolution fusion | flops 22282240 | bytes 5374976 | tf_op jit(solution)/shard_map/vhtu,uvhd->tvhd/dot_general | solution.py:33
  512.7 3.4 copy.32
  516.1 0.8 reshape.113
  517.0 0.6 fusion.36
  517.5 0.6 multiply_reduce_fusion
  518.2 1.3 fusion.6
  519.5 12.8 %all_to_all.29 = bf16[32,1,64,128]{3,2,1,0:T(8,128)(2,1)S(1)} all-to-all(bf16[32,1,64,128]{3,2,1,0:T(8,128)(2,1)S(1)} %bitcast.69), channel_id=1, replica_groups=mesh['tm'=8,'vert'=32] {'tm'}, dimensions={0} | all-to-all | bytes 1048576 | tf_op jit(solution)/shard_map/all_to_all | solution.py:92
  532.3 0.8 copy.34
  (28 shorter events, 0.1 us)
Async XLA Ops:
  0.0 518.2 %copy-start = (bf16[512,128]{1,0:T(8,128)(2,1)S(1)}, bf16[512,128]{1,0:T(8,128)(2,1)}, u32[]{:S(2)}) copy-start(bf16[512,128]{1,0:T(8,128)(2,1)} %param.19) | copy-start | bytes 393220
  7.1 11.8 %copy-start.8 = (s32[4,4,8]{2,1,0:T(4,128)S(1)}, s32[4,4,8]{2,1,0:T(4,128)}, u32[]{:S(2)}) copy-start(s32[4,4,8]{2,1,0:T(4,128)} %param.11) | copy-start | bytes 1540
  7.1 418.5 %all-to-all-start = ((bf16[32,4,512,128]{3,2,1,0:T(8,128)(2,1)}), bf16[32,4,512,128]{3,2,1,0:T(8,128)(2,1)}, u32[]{:S(2)}, u32[]{:S(2)}) async-start(bf16[32,4,512,128]{3,2,1,0:T(8,128)(2,1)} %stack.2), calls=%async_computation | async-start | bytes 33554432 | tf_op jit(solution)/shard_map/all_to_all | solution.py:57
  448.4 4.8 copy-start.7
  448.4 10.4 %copy-start.9 = (bf16[32,128]{1,0:T(8,128)(2,1)S(1)}, bf16[32,128]{1,0:T(8,128)(2,1)}, u32[]{:S(2)}) copy-start(bf16[32,128]{1,0:T(8,128)(2,1)} %param.14) | copy-start | bytes 24580
  453.2 16.9 %copy-start.5 = (bf16[128,384]{1,0:T(8,128)(2,1)S(1)}, bf16[128,384]{1,0:T(8,128)(2,1)}, u32[]{:S(2)}) copy-start(bf16[128,384]{1,0:T(8,128)(2,1)} %param.15) | copy-start | bytes 294916
  454.3 14.8 %all-to-all-start.1 = ((bf16[4,8,64,128]{3,2,0,1:T(8,128)(2,1)}), bf16[4,8,64,128]{3,2,0,1:T(8,128)(2,1)S(1)}, u32[]{:S(2)}, u32[]{:S(2)}) async-start(bf16[4,8,64,128]{3,2,0,1:T(8,128)(2,1)} %copy.26), calls=%async_computation.1 | async-start | bytes 1048576 | tf_op jit(solution)/shard_map/all_to_all | solution.py:87
  469.3 0.8 copy-start.1
  478.7 9.1 %copy-start.3 = (bf16[32,64,1,16,8]{1,0,4,3,2:T(8,128)(2,1)S(1)}, bf16[32,64,1,16,8]{1,0,4,3,2:T(8,128)(2,1)}, u32[]{:S(2)}) copy-start(bf16[32,64,1,16,8]{1,0,4,3,2:T(8,128)(2,1)} %get-tuple-element.5) | copy-start | bytes 1572868
  491.8 11.1 %copy-start.4 = (bf16[32,64,1,16,8]{0,4,3,1,2:T(8,128)(2,1)S(1)}, bf16[32,64,1,16,8]{0,4,3,1,2:T(8,128)(2,1)}, u32[]{:S(2)}) copy-start(bf16[32,64,1,16,8]{0,4,3,1,2:T(8,128)(2,1)} %copy.37) | copy-start | bytes 1572868
  512.7 4.2 copy-start.2
  512.7 4.2 copy-start.6
  512.7 5.5 %copy-start.10 = (bf16[128,512]{1,0:T(8,128)(2,1)S(1)}, bf16[128,512]{1,0:T(8,128)(2,1)}, u32[]{:S(2)}) copy-start(bf16[128,512]{1,0:T(8,128)(2,1)} %param.18) | copy-start | bytes 393220
  512.7 5.5 %copy-start.11 = (f32[128]{0:T(128)S(1)}, f32[128]{0:T(128)}, u32[]{:S(2)}) copy-start(f32[128]{0:T(128)} %param.17) | copy-start | bytes 1540
